TPU v7x, 256 devices: a whole 4x4x8 slice. The times are simulated.
256 devices in a mesh: slab: 64 (over x, z, core), img: 4 (over y).
Axes of the slice: x: 4, y: 4, z: 8, core: 2. Of those that a mesh axis runs over, the one named last changes fastest.
Arguments:
- volume: bfloat16 [32768, 256], P('slab'), may hold values from -6 to 6
- interp: bfloat16 [4, 64, 16, 32768], P('img', None, None, 'slab'), may hold values from -0.09375 to 0.09375
- block_index: int32 [4, 64, 64], P('img'), may hold values from 0 to 7
- images: bfloat16 [4, 1024, 128, 256], P('img', 'slab'), may hold values from -6 to 6
- defocus: float32 [4, 1024], P('img', 'slab'), may hold values from 5000 to 25000
- orient: int32 [4, 1024, 4], P('img', 'slab'), may hold values from 0 to 63, all different within a row
Outputs:
- update: float32 [32768, 256], P('slab')
- weights: float32 [4, 1024, 64], P('img', 'slab')
Inputs may be any that keep to these rules, and one draw needn't show every extreme that they name: `orient`: each image lists 4 different orientations of its group.
All inputs are finite; a program needn't handle non-finite values.
Results may differ from a plain program's by a relative error of at most 0.0077.
Values may be sent and summed in bfloat16 or wider, within the bound.
A program may use at most 64 MiB of HBM per device.

v0:
```python
import math
import jax
import jax.numpy as jnp
from jax import lax
from jax.sharding import PartitionSpec as P

BOX = 256
NS = 16
wave_length = 0.0197
aberration = 27000000.0
amplitude = 0.1
grid_side = 4


def phase_tables(fourier, shifts, box):
    freq = (jnp.arange(fourier, dtype=jnp.int32) - fourier // 2).astype(jnp.float32)
    shift_steps = jnp.arange(shifts, dtype=jnp.int32)
    shift_x = (2 * (shift_steps // grid_side) - (grid_side - 1)).astype(jnp.float32)
    shift_y = (2 * (shift_steps % grid_side) - (grid_side - 1)).astype(jnp.float32)
    angle = 2.0 * math.pi / box * (freq[:, None, None] * shift_x + freq[None, :, None] * shift_y)
    forward = jnp.stack([jnp.cos(angle), jnp.sin(angle)], axis=1).reshape(
        2 * fourier * fourier, shifts
    )
    backward = jnp.stack([jnp.cos(angle), -jnp.sin(angle)], axis=1).reshape(
        2 * fourier * fourier, shifts
    )
    return (forward.astype(jnp.bfloat16), backward.T.astype(jnp.bfloat16))


def contrast(defocus_blk, fourier, box):
    freq = (jnp.arange(fourier, dtype=jnp.int32) - fourier // 2).astype(jnp.float32)
    wave_sq = (freq[:, None] * freq[:, None] + freq[None, :] * freq[None, :]) / (box * box)
    phase = math.pi * wave_length * defocus_blk[:, None, None] * wave_sq
    phase = phase - 0.5 * math.pi * aberration * wave_length**3 * wave_sq * wave_sq
    return -(math.sqrt(1.0 - amplitude * amplitude) * jnp.sin(phase) + amplitude * jnp.cos(phase))


def correlate(panels, image_blk, list_blk, defocus_blk, phase_fwd, phase_back, box):
    count = image_blk.shape[0]
    fourier = image_blk.shape[1]
    picks = list_blk.shape[1]
    shifts = phase_fwd.shape[1]
    ctf = contrast(defocus_blk, fourier, box)
    weighted = ctf[:, :, None, :] * image_blk.astype(jnp.float32).reshape(
        count, fourier, 2, fourier
    )
    real_u = weighted[:, None, :, 0]
    imag_u = weighted[:, None, :, 1]
    chosen = panels[list_blk].astype(jnp.float32).reshape(count, picks, fourier, 2, fourier)
    real_p = chosen[:, :, :, 0]
    imag_p = chosen[:, :, :, 1]
    product = jnp.stack(
        [real_p * real_u + imag_p * imag_u, real_p * imag_u - imag_p * real_u], axis=3
    )
    product = product.astype(jnp.bfloat16).reshape(count * picks, 2 * fourier * fourier)
    scores = jnp.dot(product, phase_fwd, preferred_element_type=jnp.float32) / fourier
    scores = scores.reshape(count, picks * shifts)
    squared = scores * scores
    weights = squared / (jnp.mean(squared, axis=1, keepdims=True) + 1e-05)
    rounded = weights.astype(jnp.bfloat16).reshape(count * picks, shifts)
    spread = jnp.dot(rounded, phase_back, preferred_element_type=jnp.float32)
    spread = spread.reshape(count, picks, fourier, 2, fourier)
    real_e = spread[:, :, :, 0]
    imag_e = spread[:, :, :, 1]
    backed = jnp.stack(
        [real_u * real_e - imag_u * imag_e, real_u * imag_e + imag_u * real_e], axis=3
    )
    backed = backed.astype(jnp.bfloat16).reshape(count * picks, 2 * fourier * fourier)
    return (weights, backed)


def on_device(volume, interp, block_index, images, defocus, orient):
    slab_count = lax.axis_size("slab")
    slab_index = lax.axis_index("slab")
    orient_count = interp.shape[1]
    ori_dev = orient_count // slab_count
    block_rows = interp.shape[2]
    fourier = images.shape[2]
    block_count = fourier // block_rows
    img_dev = images.shape[1]
    picks = orient.shape[2]
    levels = jnp.arange(block_count, dtype=jnp.int32)
    partial_value = jnp.einsum("jpr,rx->jpx", interp[0], volume, preferred_element_type=jnp.float32)
    own_blocks = lax.dynamic_index_in_dim(block_index[0], slab_index, axis=1, keepdims=False)
    owned_idx = lax.dynamic_slice_in_dim(block_index[0], slab_index * ori_dev, ori_dev, 0)
    chosen = (own_blocks[:, None] == levels[None, :]).astype(jnp.float32)
    summed = lax.psum_scatter(
        (chosen[:, :, None, None] * partial_value[:, None]).reshape(
            lax.axis_size("slab") * ori_dev, fourier, 2 * fourier
        ),
        "slab",
        scatter_dimension=0,
        tiled=True,
    )
    panels = lax.all_gather(summed.astype(jnp.bfloat16), "slab", axis=0, tiled=True)
    phase_fwd, phase_back = phase_tables(fourier, NS, BOX)
    blk = math.gcd(img_dev, 32)
    blk_total = img_dev // blk

    def per_block(pieces):
        image_blk, list_blk, defocus_blk = pieces
        return correlate(panels, image_blk, list_blk, defocus_blk, phase_fwd, phase_back, BOX)

    weights, backs = lax.map(
        per_block,
        (
            images[0].reshape(blk_total, blk, fourier, 2 * fourier),
            orient[0].reshape(blk_total, blk, picks),
            defocus[0].reshape(blk_total, blk),
        ),
    )
    all_slices = backs.reshape(img_dev * picks, 2 * fourier * fourier)
    member = (
        orient[0].reshape(-1)[:, None] == jnp.arange(orient_count, dtype=jnp.int32)[None, :]
    ).astype(jnp.bfloat16)
    back_own = lax.psum_scatter(
        lax.dot_general(
            member, all_slices, (((0,), (0,)), ((), ())), preferred_element_type=jnp.float32
        ),
        "slab",
        scatter_dimension=0,
        tiled=True,
    ).astype(jnp.bfloat16)
    back_own = back_own.reshape(ori_dev, block_count, block_rows, 2 * fourier)
    chosen_back = (owned_idx[:, :, None] == levels).astype(jnp.bfloat16)
    outgoing = jnp.einsum(
        "osb,obpx->sopx", chosen_back, back_own, preferred_element_type=jnp.float32
    )
    outgoing = outgoing.astype(jnp.bfloat16).reshape(slab_count * ori_dev, block_rows, 2 * fourier)
    incoming = lax.all_to_all(outgoing, "slab", split_axis=0, concat_axis=0, tiled=True)
    column = jnp.einsum("jpr,jpx->rx", interp[0], incoming, preferred_element_type=jnp.float32)
    summed_cols = lax.psum(column, "img")
    update = summed_cols / math.sqrt(img_dev * slab_count)
    return (update, weights)


def solution(mesh):
    return jax.shard_map(
        on_device,
        mesh=mesh,
        in_specs=(
            P("slab", None),
            P("img", None, None, "slab"),
            P("img", None, None),
            P("img", "slab", None, None),
            P("img", "slab"),
            P("img", "slab", None),
        ),
        out_specs=(P("slab", None), P("img", "slab", None)),
        check_vma=False,
    )
```

profile of v0, /device:TPU:2, one launch (start us, length us, event | category | flops | bytes accessed | tf_op | source)
XLA Modules:
  0.0 703.3 jit_solution(17142144156621512723)
XLA Ops:
  7.2 0.0 reduce-scatter.2.cloned.1.call-start
  7.2 1.0 dynamic-slice_reduce_fusion
  8.3 0.1 copy.51
  8.3 0.1 copy-done
  8.4 1.4 fusion.7
  9.8 3.9 bitcast_multiply_fusion
  13.7 0.0 reduce-scatter.2.cloned.1.call-update
  13.7 0.0 all-gather.2.cloned.1.call-start
  13.7 153.4 %reduce-scatter.2.cloned.1.call-done = f32[1,128,256]{2,1,0:T(8,128)} async-done(((f32[64,128,256]{2,1,0:T(8,128)}), f32[1,128,256]{2,1,0:T(8,128)}) %reduce-scatter.2.cloned.1.call-update) | async-done | bytes 131088 | tf_op jit(solution)/shard_map/reduce_scatter | solution.py:87
  167.2 1.5 convert_element_type.137
  168.7 0.0 all-gather.2.cloned.1.call-update
  168.7 0.0 all-reduce.4.cloned.1.call-start
  168.8 0.1 copy.49
  168.9 0.1 copy.52
  169.0 0.1 reshape.431
  169.1 2.1 reshape.427
  171.2 0.1 broadcast_multiply_fusion.2
  171.3 0.1 copy.57
  171.4 5.4 fusion.10
  176.7 0.8 copy-done.2
  177.5 0.1 pad_maximum_fusion.3
  177.6 1.9 copy.58
  179.6 2.6 convert_element_type.143
  182.2 0.1 eq.69
  182.3 0.6 dynamic-slice.2
  182.9 0.7 dynamic-slice_bitcast_fusion
  183.6 0.1 add_multiply_fusion.2
  183.7 3.9 add_negate_fusion
  187.5 1.2 copy_multiply_fusion
  188.8 1.1 slice_bitcast_fusion.1
  189.9 57.4 %all-gather.2.cloned.1.call-done = bf16[64,128,256]{2,1,0:T(8,128)(2,1)} async-done(((bf16[1,128,256]{2,1,0:T(8,128)(2,1)}), bf16[64,128,256]{2,1,0:T(8,128)(2,1)}) %all-gather.2.cloned.1.call-update) | async-done | bytes 4194320 | tf_op jit(solution)/shard_map/all_gather | solution.py:95
  247.3 4.9 gather_fusion
  252.2 7.0 copy.53
  259.2 7.8 %fusion.30 = (f32[16,4,128,1,128]{2,4,3,1,0:T(8,128)}, f32[16,4,128,1,128]{2,4,3,1,0:T(8,128)}) fusion(f32[16,4,128,2,128]{2,4,3,1,0:T(8,128)} %bitcast.54), kind=kLoop, calls=%fused_computation.71 | loop fusion | bytes 16777216 | tf_op jit(solution)/shard_map/while/body/eval_jaxpr/slice | solution.py:50
  267.0 5.5 copy.73
  272.5 5.5 copy.74
  277.9 4.9 add_convert_fusion.1
  282.9 0.4 pad_maximum_fusion
  283.2 6.6 copy.56
  289.8 7.8 %convert_element_type.140 = bf16[64,32768]{1,0:T(8,128)(2,1)} reshape(bf16[16,4,128,2,128]{4,3,2,1,0:T(2,128)(2,1)} %copy.56) | data formatting | bytes 8388608 | tf_op jit(solution)/shard_map/while/body/eval_jaxpr/convert_element_type | solution.py:55
  297.6 3.7 fusion.31
  301.4 0.1 reduce_sum.18
  301.4 0.1 reduce_sum.19
  301.6 0.1 div.67
  301.6 0.1 div.68
  301.8 0.1 copy.59
  301.9 2.4 fusion.3
  304.2 1.5 subtract_convert_fusion
  305.7 0.4 pad_maximum_fusion.1
  306.1 6.5 copy.61
  312.7 7.9 %convert_element_type.145 = bf16[64,32768]{1,0:T(8,128)(2,1)} reshape(bf16[16,4,128,2,128]{4,3,2,1,0:T(2,128)(2,1)} %copy.61) | data formatting | bytes 8388608 | tf_op jit(solution)/shard_map/while/body/eval_jaxpr/convert_element_type | solution.py:68
  320.5 6.8 fusion.15
  327.3 257.5 %all-reduce.5 = bf16[64,32768]{1,0:T(8,128)(2,1)} all-reduce(f32[64,32768]{1,0:T(8,128)} %fusion.15), channel_id=3, replica_groups=mesh['slab'=64,'img'=4] {'slab'}, use_global_device_ids=true, to_apply=%region_3.4.clone | all-reduce | flops 2097152 | bytes 12582912
  584.8 2.1 fusion.12
  586.9 0.3 fusion
  587.3 0.3 copy.63
  587.6 59.8 %all_to_all.5 = bf16[64,16,256]{2,1,0:T(8,128)(2,1)S(1)} all-to-all(bf16[64,16,256]{2,1,0:T(8,128)(2,1)S(1)} %copy.63), channel_id=1, replica_groups=mesh['slab'=64,'img'=4] {'slab'}, dimensions={0} | all-to-all | bytes 1048576 | tf_op jit(solution)/shard_map/all_to_all | solution.py:130
  647.3 1.2 convolution_bitcast_fusion
  648.6 0.1 copy.66
  648.7 0.1 mul.372
  648.8 0.7 broadcast_divide_fusion
  649.4 45.2 %all-reduce.4.cloned.1.call-done = f32[512,256]{0,1:T(8,128)} async-done(((f32[512,256]{0,1:T(8,128)}), f32[512,256]{0,1:T(8,128)}) %all-reduce.4.cloned.1.call-update) | async-done | bytes 524304 | tf_op jit(solution)/shard_map/psum | solution.py:132
  694.7 1.1 broadcast_multiply_fusion
  695.7 1.0 copy.67
  (24 shorter events, 0.1 us)
Async XLA Ops:
  7.2 1.2 copy-start
  7.2 160.0 %reduce-scatter.2.cloned.1.call-start = ((), (), s32[]{:S(2)}) async-start(), calls=%async_computation.2 | async-start | bytes 8519680 | tf_op jit(solution)/shard_map/reduce_scatter | solution.py:87
  13.7 155.1 %copy-start.4 = (s32[1,16,4]{1,2,0:T(4,128)S(1)}, s32[1,16,4]{1,2,0:T(4,128)}, u32[]{:S(2)}) copy-start(s32[1,16,4]{1,2,0:T(4,128)} %param.11) | copy-start | bytes 772
  13.7 233.6 %all-gather.2.cloned.1.call-start = ((), (), s32[]{:S(2)}) async-start(), calls=%async_computation.3 | async-start | bytes 4259840 | tf_op jit(solution)/shard_map/all_gather | solution.py:95
  168.7 525.9 %all-reduce.4.cloned.1.call-start = ((), (), s32[]{:S(2)}) async-start(), calls=%async_computation.4 | async-start | bytes 1048576 | tf_op jit(solution)/shard_map/psum | solution.py:132
  171.1 11.1 %copy-start.6 = (u32[256]{0:T(256)S(1)}, u32[256]{0:T(256)}, u32[]{:S(2)}) copy-start(u32[256]{0:T(256)} %constant.117) | copy-start | bytes 3076
  171.2 12.4 %copy-start.5 = (f32[1,16]{1,0:T(1,128)S(1)}, f32[1,16]{1,0:T(1,128)}, u32[]{:S(2)}) copy-start(f32[1,16]{1,0:T(1,128)} %param.10) | copy-start | bytes 196
  176.7 0.8 copy-start.2
  297.6 4.3 copy-start.3
  301.9 2.4 copy-start.1
Sparse Core Ops, SparseCore 0:
  13.8 153.3 reduce-scatter.1
  170.3 76.9 all-gather.1
  648.7 45.8 all-reduce.3
where the time goes:
time: 704 us; the launch traced here: 703 us
  blocking collectives  317 us (45%)
  waiting for transfers between devices  256 us (36%)
  local copies, waits for them, and re-layouts  74.8 us (11%)
  other arithmetic  25.2 us (4%)
  matrix products  15.8 us (2%)
  between operations  14 us (2%)
    unnamed x1, blocking collectives  257 us
    reduce_scatter x1, waiting for transfers between devices, on_device(): lax.psum_scatter((chosen[:, :, None, None] * partial_value[:, None]).resh...  153 us
    all_to_all x1, blocking collectives, on_device(): lax.all_to_all(outgoing, 'slab', split_axis=0, concat_axis=0, tiled=True)  59.8 us
    all_gather x1, waiting for transfers between devices, on_device(): lax.all_gather(summed.astype(jnp.bfloat16), 'slab', axis=0, tiled=True)  57.4 us
    psum x1, waiting for transfers between devices, on_device(): summed_cols = lax.psum(column, 'img')  45.2 us
  transfers between devices with their start and end apart: 3, of which 3 were waited for; matrix products, arithmetic and copies ran while one was open for 3% of the time, Pallas kernels for 0%

commit v1 on v0

--- a/solution.py
+++ b/solution.py
@@ -3,6 +3,7 @@
 import jax.numpy as jnp
 from jax import lax
 from jax.sharding import PartitionSpec as P
+from jax.lax import all_to_all, axis_size
 
 BOX = 256
 NS = 16
@@ -70,6 +71,18 @@
 
 
 def on_device(volume, interp, block_index, images, defocus, orient):
+
+    def refer_the_limits(local_array):
+        return jnp.concatenate(
+            all_to_all(
+                jnp.stack([local_array for _ in range(axis_size("slab"))], axis=0),
+                axis_name="slab",
+                split_axis=0,
+                concat_axis=0,
+            ),
+            axis=0,
+        )
+
     slab_count = lax.axis_size("slab")
     slab_index = lax.axis_index("slab")
     orient_count = interp.shape[1]
@@ -92,7 +105,7 @@
         scatter_dimension=0,
         tiled=True,
     )
-    panels = lax.all_gather(summed.astype(jnp.bfloat16), "slab", axis=0, tiled=True)
+    panels = refer_the_limits(summed.astype(jnp.bfloat16))
     phase_fwd, phase_back = phase_tables(fourier, NS, BOX)
     blk = math.gcd(img_dev, 32)
     blk_total = img_dev // blk

time: 704 us -> 729 us (1.036)
  waiting for transfers between devices: 256 us -> 272 us
  starting transfers between devices: 0.12 us -> 8.88 us
    all_to_all x0 -> x1, waiting for transfers between devices: none -> 73.4 us  [refer_the_limits(): all_to_all(jnp.stack([local_array for _ in range(axis_size('slab'))], axi...]
    all_gather x1 -> x0, waiting for transfers between devices: 57.4 us -> none  [on_device(): lax.all_gather(summed.astype(jnp.bfloat16), 'slab', axis=0, tiled=True)]
    all_to_all x0 -> x1, starting transfers between devices: none -> 8.61 us  [refer_the_limits(): all_to_all(jnp.stack([local_array for _ in range(axis_size('slab'))], axi...]
where the time goes in v1:
time: 729 us; the launch traced here: 728 us
  blocking collectives  315 us (43%)
  waiting for transfers between devices  272 us (37%)
  local copies, waits for them, and re-layouts  77.3 us (11%)
  other arithmetic  24.6 us (3%)
  matrix products  15.8 us (2%)
  between operations  14.3 us (2%)
  starting transfers between devices  8.88 us (1%)
    unnamed x1, blocking collectives  256 us
    reduce_scatter x1, waiting for transfers between devices, on_device(): lax.psum_scatter((chosen[:, :, None, None] * partial_value[:, None]).resh...  153 us
    all_to_all x1, waiting for transfers between devices, refer_the_limits(): all_to_all(jnp.stack([local_array for _ in range(axis_size('slab'))], axi...  73.4 us
    all_to_all x1, blocking collectives, on_device(): lax.all_to_all(outgoing, 'slab', split_axis=0, concat_axis=0, tiled=True)  59.3 us
    psum x1, waiting for transfers between devices, on_device(): summed_cols = lax.psum(column, 'img')  45.1 us
  transfers between devices with their start and end apart: 3, of which 3 were waited for; matrix products, arithmetic and copies ran while one was open for 3% of the time, Pallas kernels for 0%

profile of v1, /device:TPU:2, one launch (start us, length us, event | category | flops | bytes accessed | tf_op | source)
XLA Modules:
  0.0 727.9 jit_solution(18114812535091587456)
XLA Ops:
  7.2 0.0 reduce-scatter.2.cloned.1.call-start
  7.2 1.0 dynamic-slice_reduce_fusion
  8.3 0.1 copy.51
  8.3 0.1 copy-done
  8.4 1.4 fusion.7
  9.8 3.9 bitcast_multiply_fusion
  13.7 0.0 reduce-scatter.2.cloned.1.call-update
  13.7 153.5 %reduce-scatter.2.cloned.1.call-done = f32[1,128,256]{2,1,0:T(8,128)} async-done(((f32[64,128,256]{2,1,0:T(8,128)}), f32[1,128,256]{2,1,0:T(8,128)}) %reduce-scatter.2.cloned.1.call-update) | async-done | bytes 131088 | tf_op jit(solution)/shard_map/reduce_scatter | solution.py:100
  167.2 0.9 convert_bitcast_fusion
  168.1 2.5 stack.20
  170.5 8.6 %all-to-all-start = ((bf16[64,1,128,256]{3,2,1,0:T(8,128)(2,1)}), bf16[64,1,128,256]{3,2,1,0:T(8,128)(2,1)}, u32[]{:S(2)}, u32[]{:S(2)}) async-start(bf16[64,1,128,256]{3,2,1,0:T(8,128)(2,1)} %stack.20), calls=%async_computation.1 | async-start | bytes 8388608 | tf_op jit(solution)/shard_map/all_to_all | solution.py:77
  179.2 0.2 all-reduce.4.cloned.1.call-start
  179.4 0.1 copy.49
  179.5 0.1 copy.52
  179.6 0.1 reshape.438
  179.7 2.1 reshape.434
  181.8 0.1 broadcast_multiply_fusion.2
  181.9 0.1 copy.57
  182.0 5.4 fusion.10
  187.4 0.8 copy-done.2
  188.2 0.1 pad_maximum_fusion.3
  188.3 2.0 copy.58
  190.3 2.6 convert_element_type.146
  192.9 0.1 eq.69
  193.0 0.6 dynamic-slice.2
  193.6 0.7 dynamic-slice_bitcast_fusion
  194.3 0.1 add_multiply_fusion.2
  194.4 3.9 add_negate_fusion
  198.2 1.2 copy_multiply_fusion
  199.5 1.1 slice_bitcast_fusion.1
  200.6 73.4 %all-to-all-done = bf16[64,1,128,256]{3,2,1,0:T(8,128)(2,1)} async-done(((bf16[64,1,128,256]{3,2,1,0:T(8,128)(2,1)}), bf16[64,1,128,256]{3,2,1,0:T(8,128)(2,1)}, u32[]{:S(2)}, u32[]{:S(2)}) %all-to-all-start) | async-done | bytes 4194336 | tf_op jit(solution)/shard_map/all_to_all | solution.py:77
  274.0 4.9 gather_fusion
  279.0 7.0 copy.53
  286.0 7.8 %fusion.30 = (f32[16,4,128,1,128]{2,4,3,1,0:T(8,128)}, f32[16,4,128,1,128]{2,4,3,1,0:T(8,128)}) fusion(f32[16,4,128,2,128]{2,4,3,1,0:T(8,128)} %bitcast.57), kind=kLoop, calls=%fused_computation.72 | loop fusion | bytes 16777216 | tf_op jit(solution)/shard_map/while/body/eval_jaxpr/slice | solution.py:51
  293.8 5.5 copy.73
  299.2 5.5 copy.74
  304.7 4.9 add_convert_fusion.1
  309.6 0.4 pad_maximum_fusion
  310.0 6.6 copy.56
  316.6 7.8 %convert_element_type.143 = bf16[64,32768]{1,0:T(8,128)(2,1)} reshape(bf16[16,4,128,2,128]{4,3,2,1,0:T(2,128)(2,1)} %copy.56) | data formatting | bytes 8388608 | tf_op jit(solution)/shard_map/while/body/eval_jaxpr/convert_element_type | solution.py:56
  324.4 3.7 fusion.31
  328.1 0.1 reduce_sum.18
  328.2 0.1 reduce_sum.19
  328.3 0.1 div.67
  328.4 0.1 div.68
  328.5 0.1 copy.59
  328.6 2.4 fusion.3
  331.0 1.5 subtract_convert_fusion
  332.5 0.4 pad_maximum_fusion.1
  332.9 6.6 copy.61
  339.5 7.8 %convert_element_type.148 = bf16[64,32768]{1,0:T(8,128)(2,1)} reshape(bf16[16,4,128,2,128]{4,3,2,1,0:T(2,128)(2,1)} %copy.61) | data formatting | bytes 8388608 | tf_op jit(solution)/shard_map/while/body/eval_jaxpr/convert_element_type | solution.py:69
  347.3 6.8 fusion.15
  354.1 255.6 %all-reduce.5 = bf16[64,32768]{1,0:T(8,128)(2,1)} all-reduce(f32[64,32768]{1,0:T(8,128)} %fusion.15), channel_id=3, replica_groups=mesh['slab'=64,'img'=4] {'slab'}, use_global_device_ids=true, to_apply=%region_3.4.clone | all-reduce | flops 2097152 | bytes 12582912
  609.6 2.1 fusion.12
  611.8 0.3 fusion
  612.1 0.3 copy.63
  612.4 59.3 %all_to_all.10 = bf16[64,16,256]{2,1,0:T(8,128)(2,1)S(1)} all-to-all(bf16[64,16,256]{2,1,0:T(8,128)(2,1)S(1)} %copy.63), channel_id=1, replica_groups=mesh['slab'=64,'img'=4] {'slab'}, dimensions={0} | all-to-all | bytes 1048576 | tf_op jit(solution)/shard_map/all_to_all | solution.py:143
  671.8 1.2 convolution_bitcast_fusion
  673.0 0.1 copy.66
  673.1 0.1 mul.372
  673.2 0.7 broadcast_divide_fusion
  673.9 45.1 %all-reduce.4.cloned.1.call-done = f32[512,256]{0,1:T(8,128)} async-done(((f32[512,256]{0,1:T(8,128)}), f32[512,256]{0,1:T(8,128)}) %all-reduce.4.cloned.1.call-update) | async-done | bytes 524304 | tf_op jit(solution)/shard_map/psum | solution.py:145
  719.0 1.1 broadcast_multiply_fusion
  720.1 1.0 copy.67
  (24 shorter events, 0.1 us)
Async XLA Ops:
  7.2 1.2 copy-start
  7.2 160.0 %reduce-scatter.2.cloned.1.call-start = ((), (), s32[]{:S(2)}) async-start(), calls=%async_computation.3 | async-start | bytes 8519680 | tf_op jit(solution)/shard_map/reduce_scatter | solution.py:100
  170.5 8.9 %copy-start.4 = (s32[1,16,4]{1,2,0:T(4,128)S(1)}, s32[1,16,4]{1,2,0:T(4,128)}, u32[]{:S(2)}) copy-start(s32[1,16,4]{1,2,0:T(4,128)} %param.11) | copy-start | bytes 772
  170.5 103.5 %all-to-all-start = ((bf16[64,1,128,256]{3,2,1,0:T(8,128)(2,1)}), bf16[64,1,128,256]{3,2,1,0:T(8,128)(2,1)}, u32[]{:S(2)}, u32[]{:S(2)}) async-start(bf16[64,1,128,256]{3,2,1,0:T(8,128)(2,1)} %stack.20), calls=%async_computation.1 | async-start | bytes 8388608 | tf_op jit(solution)/shard_map/all_to_all | solution.py:77
  179.2 539.8 %all-reduce.4.cloned.1.call-start = ((), (), s32[]{:S(2)}) async-start(), calls=%async_computation.4 | async-start | bytes 1048576 | tf_op jit(solution)/shard_map/psum | solution.py:145
  181.8 11.2 %copy-start.6 = (u32[256]{0:T(256)S(1)}, u32[256]{0:T(256)}, u32[]{:S(2)}) copy-start(u32[256]{0:T(256)} %constant.117) | copy-start | bytes 3076
  181.8 12.5 %copy-start.5 = (f32[1,16]{1,0:T(1,128)S(1)}, f32[1,16]{1,0:T(1,128)}, u32[]{:S(2)}) copy-start(f32[1,16]{1,0:T(1,128)} %param.10) | copy-start | bytes 196
  187.4 0.8 copy-start.2
  324.4 4.3 copy-start.3
  328.6 2.4 copy-start.1
Sparse Core Ops, SparseCore 0:
  13.8 153.3 reduce-scatter.1
  673.1 45.7 all-reduce.3
